TPU v7x, 32 devices: a whole 2x2x4 slice. The times are simulated.
32 devices in a mesh: pair: 4 (over x, core), blk: 8 (over z, y).
Axes of the slice: x: 2, y: 2, z: 4, core: 2. Of those that a mesh axis runs over, the one named last changes fastest.
Arguments:
- left_feats: bfloat16 [4, 64, 256, 256], P('pair', None, 'blk'), may hold values from -6 to 6
- right_feats: bfloat16 [4, 64, 256, 256], P('pair', None, 'blk'), may hold values from -6 to 6
- offsets: int32 [8], P('blk'), may hold values from 0 to 3, as said below
- hidden: bfloat16 [4, 64, 256, 128], P('pair', None, 'blk'), may hold values from -1 to 1
- context: bfloat16 [4, 3, 64, 256, 128], P('pair', None, None, 'blk'), may hold values from -6 to 6
- gru_weights: bfloat16 [2, 3, 5, 164, 128], replicated, may hold values from -0.21875 to 0.21875
- hidden_grad: float32 [4, 64, 256, 128], P('pair', None, 'blk'), may hold values from -0.06 to 0.06
Outputs:
- new_hidden: bfloat16 [4, 64, 256, 128], P('pair', None, 'blk')
- weight_grads: float32 [2, 3, 5, 164, 128], replicated
- hidden_in_grad: float32 [4, 64, 256, 128], P('pair', None, 'blk')
Inputs may be any that keep to these rules, and one draw needn't show every extreme that they name: Stripe s reads the frame-2 blocks s - offsets[s] - 1 and s - offsets[s]; some stripe has offset 4 - 1.
All inputs are finite; a program needn't handle non-finite values.
Results may differ from a plain program's by a relative error of at most 0.0054.
Values may be sent and summed in bfloat16 or wider, within the bound.
A program may use at most 128 MiB of HBM per device.

v0:
```python
import functools
import math
import jax
import jax.numpy as jnp
import numpy as np
from jax import lax
from jax.sharding import PartitionSpec as P

LEVELS = 4
RADIUS = 4


def with_halo(block, sides, width):
    for axis, dim in sides:
        count = lax.axis_size(axis)
        forward = [(i, i + 1) for i in range(count - 1)]
        backward = [(target, source) for source, target in forward]
        low = lax.ppermute(
            lax.slice_in_dim(block, block.shape[dim] - width, None, axis=dim), axis, forward
        )
        high = lax.ppermute(lax.slice_in_dim(block, 0, width, axis=dim), axis, backward)
        block = jnp.concatenate([low, block, high], axis=dim)
    return block


def lookup_table(column_count, level_count, radius_len):
    tap_count = 2 * radius_len + 1
    lookup = np.zeros((column_count, 2 * column_count, level_count * tap_count), np.float32)
    positions = np.arange(column_count)
    for level_id in range(level_count):
        pool_span = 2**level_id
        pooled_cols = 2 * column_count // pool_span
        for tap_id in range(tap_count):
            centre = (positions + column_count // 2) // pool_span + tap_id - radius_len
            inside = (centre >= 0) & (centre < pooled_cols)
            for inner_id in range(pool_span):
                lookup[
                    positions[inside],
                    centre[inside] * pool_span + inner_id,
                    level_id * tap_count + tap_id,
                ] = (1.0 / pool_span)
    return lookup


def tap_stack(padded, extent, axis_dim, kernel_len):
    return jnp.concatenate(
        [
            lax.slice_in_dim(padded, tap_id, tap_id + extent, axis=axis_dim)
            for tap_id in range(kernel_len)
        ],
        axis=-1,
    )


def conv_apply(padded, weight_taps, extent, axis_dim):
    kernel_len, in_chan, out_chan = weight_taps.shape
    stacked = tap_stack(padded, extent, axis_dim, kernel_len)
    flat_taps = stacked.reshape(-1, kernel_len * in_chan)
    result = jnp.dot(
        flat_taps,
        weight_taps.reshape(kernel_len * in_chan, out_chan),
        preferred_element_type=jnp.float32,
    )
    return result.reshape(stacked.shape[:-1] + (out_chan,))


def conv_weight_grad(padded, deltas, axis_dim):
    extent = deltas.shape[axis_dim]
    kernel_len = padded.shape[axis_dim] - extent + 1
    stacked = tap_stack(padded, extent, axis_dim, kernel_len)
    flat_taps = stacked.reshape(-1, stacked.shape[-1])
    flat_deltas = deltas.reshape(-1, deltas.shape[-1])
    result = lax.dot_general(
        flat_taps, flat_deltas, (((0,), (0,)), ((), ())), preferred_element_type=jnp.float32
    )
    return result.reshape(kernel_len, padded.shape[-1], deltas.shape[-1])


def conv_input_grad(deltas, weight_taps, axis_dim):
    kernel_len, in_chan, out_chan = weight_taps.shape
    backward_taps = lax.dot_general(
        deltas.reshape(-1, out_chan),
        weight_taps.reshape(kernel_len * in_chan, out_chan),
        (((1,), (1,)), ((), ())),
        preferred_element_type=jnp.float32,
    )
    backward_taps = backward_taps.reshape(deltas.shape[:-1] + (kernel_len * in_chan,))
    summed = None
    for tap_id in range(kernel_len):
        tap_part = backward_taps[..., tap_id * in_chan : (tap_id + 1) * in_chan]
        widths = [(0, 0)] * deltas.ndim
        widths[axis_dim] = (tap_id, kernel_len - 1 - tap_id)
        shifted = jnp.pad(tap_part, widths)
        summed = shifted if summed is None else summed + shifted
    return summed


def pad_along(values, axis_dim):
    widths = [(0, 0)] * values.ndim
    widths[axis_dim] = (2, 2)
    return jnp.pad(values, widths)


def crop_along(values, axis_dim):
    extent = values.shape[axis_dim] - 4
    return lax.slice_in_dim(values, 2, extent + 2, axis=axis_dim)


def section_forward(padded, context_parts, weights, axis_dim, extend):
    extent = padded.shape[axis_dim] - 4
    hidden_width = weights.shape[-1]
    own_inputs = lax.slice_in_dim(padded, 2, extent + 2, axis=axis_dim)
    hidden_own = own_inputs[..., :hidden_width].astype(jnp.float32)
    feat_padded = padded[..., hidden_width:]
    update_gate = jax.nn.sigmoid(
        conv_apply(padded, weights[0], extent, axis_dim) + context_parts[0].astype(jnp.float32)
    )
    reset_gate = jax.nn.sigmoid(
        conv_apply(padded, weights[1], extent, axis_dim) + context_parts[1].astype(jnp.float32)
    )
    reset_hidden = (reset_gate * hidden_own).astype(jnp.bfloat16)
    gated_padded = jnp.concatenate([extend(reset_hidden), feat_padded], axis=-1)
    candidate = jnp.tanh(
        conv_apply(gated_padded, weights[2], extent, axis_dim)
        + context_parts[2].astype(jnp.float32)
    )
    blended = (1.0 - update_gate) * hidden_own + update_gate * candidate
    return (blended, (update_gate, reset_gate, candidate, hidden_own, padded, gated_padded))


def section_backward(cotangent, stored, weights, axis_dim, fold_rims):
    update_gate, reset_gate, candidate, hidden_own, padded, gated_padded = stored
    hidden_width = weights.shape[-1]
    delta_cand = (cotangent * update_gate * (1.0 - candidate * candidate)).astype(jnp.bfloat16)
    grad_cand = conv_weight_grad(gated_padded, delta_cand, axis_dim)
    back_gated = fold_rims(conv_input_grad(delta_cand, weights[2][:, :hidden_width], axis_dim))
    delta_update = (
        cotangent * (candidate - hidden_own) * update_gate * (1.0 - update_gate)
    ).astype(jnp.bfloat16)
    delta_reset = (back_gated * hidden_own * reset_gate * (1.0 - reset_gate)).astype(jnp.bfloat16)
    grad_update = conv_weight_grad(padded, delta_update, axis_dim)
    grad_reset = conv_weight_grad(padded, delta_reset, axis_dim)
    grad_stack = jnp.stack([grad_update, grad_reset, grad_cand])
    back_inputs = conv_input_grad(
        delta_update, weights[0][:, :hidden_width], axis_dim
    ) + conv_input_grad(delta_reset, weights[1][:, :hidden_width], axis_dim)
    hidden_back = cotangent * (1.0 - update_gate) + back_gated * reset_gate + fold_rims(back_inputs)
    return (grad_stack, hidden_back)


def extend_gated(values):
    return with_halo(values, (("blk", 1),), 2)


def stripe_rims(values):
    extent = values.shape[1] - 4
    edge_terms = jnp.concatenate([values[:, :2], values[:, extent + 2 :]], axis=1)
    arrived = with_halo(edge_terms, (("blk", 1),), 2)
    own_terms = values[:, 2 : extent + 2]
    from_left = jnp.pad(arrived[:, :2], ((0, 0), (0, extent - 2), (0, 0)))
    from_right = jnp.pad(arrived[:, 6:], ((0, 0), (extent - 2, 0), (0, 0)))
    return own_terms + from_left + from_right


def on_device(left_feats, right_feats, offsets, hidden, context, gru_weights, hidden_grad):
    left_block = left_feats[0]
    right_block = right_feats[0]
    offset = offsets[0]
    stripe = lax.axis_index("blk")
    column_count = left_block.shape[1]
    empty_block = jnp.zeros_like(right_block)
    low_id = stripe - offset - 1
    high_id = stripe - offset
    shards = lax.all_gather(right_block, "blk", axis=1, tiled=True)
    shard_cols = shards.shape[1]

    def pick_one(slot_block, block_id):
        local_col = block_id * column_count
        usable = (local_col >= 0) & (local_col + column_count <= shard_cols)
        picked = lax.dynamic_slice_in_dim(
            shards, jnp.clip(local_col, 0, shard_cols - column_count), column_count, 1
        )
        return jnp.where(usable, picked, slot_block)

    low_block = pick_one(empty_block, low_id)
    high_block = pick_one(empty_block, high_id)
    window = jnp.concatenate([low_block, high_block], axis=1)
    scores = jnp.einsum("hxc,hjc->hxj", left_block, window, preferred_element_type=jnp.float32) * (
        1.0 / math.sqrt(left_block.shape[-1])
    )
    lookup = jnp.asarray(lookup_table(column_count, LEVELS, RADIUS))
    features = jnp.einsum("hxj,xjf->hxf", scores, lookup, precision=lax.Precision.HIGHEST).astype(
        jnp.bfloat16
    )
    context_parts = context[0]
    first_inputs = jnp.concatenate([hidden[0], features], axis=-1)
    first_padded = with_halo(first_inputs, (("blk", 1),), 2)
    first_new, first_stored = section_forward(
        first_padded, context_parts, gru_weights[0], 1, extend_gated
    )
    first_hidden = first_new.astype(jnp.bfloat16)
    second_inputs = jnp.concatenate([first_hidden, features], axis=-1)
    second_new, second_stored = section_forward(
        pad_along(second_inputs, 0),
        context_parts,
        gru_weights[1],
        0,
        functools.partial(pad_along, axis_dim=0),
    )
    second_grads, first_back = section_backward(
        hidden_grad[0], second_stored, gru_weights[1], 0, functools.partial(crop_along, axis_dim=0)
    )
    first_grads, hidden_back = section_backward(
        first_back, first_stored, gru_weights[0], 1, stripe_rims
    )
    grad_stack = lax.psum(jnp.stack([first_grads, second_grads]), ("pair", "blk"))
    return (second_new.astype(jnp.bfloat16)[None], grad_stack, hidden_back[None])


def solution(mesh):
    placed = (
        P("pair", None, "blk", None),
        P("pair", None, "blk", None),
        P("blk"),
        P("pair", None, "blk", None),
        P("pair", None, None, "blk", None),
        P(),
        P("pair", None, "blk", None),
    )
    return jax.shard_map(
        on_device,
        mesh=mesh,
        in_specs=placed,
        out_specs=(P("pair", None, "blk", None), P(), P("pair", None, "blk", None)),
        check_vma=False,
    )
```

profile of v0, /device:TPU:0, one launch (start us, length us, event | category | flops | bytes accessed | tf_op | source)
XLA Modules:
  0.0 494.4 jit_solution(1043420342084576107)
XLA Ops:
  8.6 129.2 %all-gather.3.cloned.1.call-done = bf16[1,64,256,256]{3,2,1,0:T(8,128)(2,1)} async-done(((bf16[1,64,32,256]{3,2,1,0:T(8,128)(2,1)}), bf16[1,64,256,256]{3,2,1,0:T(8,128)(2,1)}) %all-gather.3.cloned.1.call-update) | async-done | bytes 8388624 | tf_op jit(solution)/shard_map/all_gather | solution.py:174
  137.9 2.8 select_bitcast_fusion.1
  141.7 2.5 fusion.30
  146.6 4.5 collective-permute-start
  151.1 2.8 fusion.78
  155.8 2.7 fusion.76
  158.5 7.6 %concatenate.75 = bf16[64,32,820]{2,1,0:T(8,128)(2,1)} concatenate(bf16[64,32,164]{2,1,0:T(8,128)(2,1)} %get-tuple-element.86, bf16[64,32,164]{2,1,0:T(8,128)(2,1)} %get-tuple-element.87, bf16[64,32,128]{2,1,0:T(8,128)(2,1)S(1)} %bitcast.177, bf16[64,32,36]{2,1,0:T(8,128)(2,1)S(1)} %copy.20, bf16[64,32,164]{2,1,0:T(8,128)(2,1)S(1)} %get-tuple-element.56, ...), dimensions={2} | concatenate | bytes 6717440 | tf_op jit(solution)/shard_map/concatenate | solution.py:46
  166.1 4.4 fusion.34
  172.5 5.6 %collective-permute-start.2 = (bf16[64,2,128]{2,1,0:T(2,128)(2,1)}, bf16[64,2,128]{2,1,0:T(2,128)(2,1)}, u32[]{:S(2)}, u32[]{:S(2)}) collective-permute-start(bf16[64,2,128]{2,1,0:T(2,128)(2,1)} %get-tuple-element.78), channel_id=1, source_target_pairs={{0,1},{1,2},{2,3},{3,4},{4,5},{5,6},{6,7},{8,9},{9,10},{10,11},{11... | collective-permute-start | bytes 98312 | tf_op jit(solution)/shard_map/ppermute | solution.py:18
  201.7 7.6 %concatenate.90 = bf16[2048,820]{1,0:T(8,128)(2,1)} concatenate(bf16[2048,164]{1,0:T(8,128)(2,1)} %bitcast.185, bf16[2048,164]{1,0:T(8,128)(2,1)} %bitcast.186, bf16[2048,128]{1,0:T(8,128)(2,1)S(1)} %bitcast.178, bf16[2048,36]{1,0:T(8,128)(2,1)S(1)} %bitcast.173, bf16[2048,164]{1,0:T(8,128)(2,1)S(1)} %bitcast.184, bf16[2048,164]{1,0:T(8,128)(2,1)S(1)} %bitcast.183), dimensions={1} | concatenate | bytes 6717440 | tf_op jit(solution)/shard_map/concatenate | solution.py:46
  209.3 6.0 %copy.32 = bf16[820,2048]{1,0:T(8,128)(2,1)} copy(bf16[820,2048]{0,1:T(8,128)(2,1)} %bitcast.182) | data formatting | bytes 6717440 | tf_op jit(solution)/shard_map/dot_general | solution.py:73
  215.4 4.3 reshape.193
  221.2 2.8 fusion.75
  224.0 8.0 %concatenate.79 = bf16[64,32,820]{2,1,0:T(8,128)(2,1)} concatenate(bf16[64,32,164]{2,1,0:T(8,128)(2,1)} %get-tuple-element.54, bf16[64,32,164]{2,1,0:T(8,128)(2,1)} %get-tuple-element.53, bf16[64,32,164]{2,1,0:T(8,128)(2,1)} %get-tuple-element.52, bf16[64,32,164]{2,1,0:T(8,128)(2,1)S(1)} %get-tuple-element.51, bf16[64,32,164]{2,1,0:T(8,128)(2,1)S(1)} %get-tuple-element.50), dimensions={2} | concatenate | bytes 6717440 | tf_op jit(solution)/shard_map/concatenate | solution.py:46
  232.0 3.4 fusion.17
  239.0 2.4 pad_slice_fusion.3
  242.4 8.3 %concatenate.81 = bf16[64,32,820]{2,1,0:T(8,128)(2,1)} concatenate(bf16[64,32,164]{2,1,0:T(8,128)(2,1)} %get-tuple-element.73, bf16[64,32,164]{2,1,0:T(8,128)(2,1)} %get-tuple-element.71, bf16[64,32,128]{2,1,0:T(8,128)(2,1)} %copy-done.22, bf16[64,32,36]{2,1,0:T(8,128)(2,1)S(1)} %copy.20, bf16[64,32,164]{2,1,0:T(8,128)(2,1)} %get-tuple-element.72, ...), dimensions={2} | concatenate | bytes 6717440 | tf_op jit(solution)/shard_map/concatenate | solution.py:46
  250.6 4.5 fusion.16
  255.2 3.3 fusion.44
  261.1 8.5 %concatenate.83 = bf16[64,32,820]{2,1,0:T(8,128)(2,1)} concatenate(bf16[64,32,164]{2,1,0:T(8,128)(2,1)} %get-tuple-element.69, bf16[64,32,164]{2,1,0:T(8,128)(2,1)} %get-tuple-element.68, bf16[64,32,164]{2,1,0:T(8,128)(2,1)} %get-tuple-element.67, bf16[64,32,164]{2,1,0:T(8,128)(2,1)} %get-tuple-element.66, bf16[64,32,164]{2,1,0:T(8,128)(2,1)} %get-tuple-element.65), dimensions={2} | concatenate | bytes 6717440 | tf_op jit(solution)/shard_map/concatenate | solution.py:46
  269.7 5.3 %fusion.48 = (bf16[64,32,128]{2,1,0:T(8,128)(2,1)S(1)}, bf16[64,32,128]{2,1,0:T(8,128)(2,1)S(1)}, bf16[1,64,32,128]{3,2,1,0:T(8,128)(2,1)}) fusion(f32[64,32,128]{2,1,0:T(8,128)} %fusion.16, bf16[64,32,128]{2,1,0:T(8,128)(2,1)S(1)} %copy-done.23, f32[1,64,32,128]{3,2,1,0:T(8,128)} %param.14, bf16[1,3,64,32,128]{4,3,2,1,0:T(8,128)(2,1)} %param.12, ...), kind=kOutput, calls=%fused_computation.80 | convolution fusion | flops 434634752 | bytes 8287232 | tf_op jit(solution)/shard_map/dot_general | solution.py:59
  290.7 6.0 %copy.35 = bf16[820,2048]{1,0:T(8,128)(2,1)} copy(bf16[820,2048]{0,1:T(8,128)(2,1)} %bitcast.181) | data formatting | bytes 6717440 | tf_op jit(solution)/shard_map/dot_general | solution.py:73
  296.7 4.2 reshape.208
  300.8 6.0 %copy.34 = bf16[820,2048]{1,0:T(8,128)(2,1)} copy(bf16[820,2048]{0,1:T(8,128)(2,1)} %bitcast.180) | data formatting | bytes 6717440 | tf_op jit(solution)/shard_map/dot_general | solution.py:73
  306.8 4.4 reshape.204
  311.3 4.0 convolution_bitcast_fusion.1
  317.1 6.0 %copy.33 = bf16[820,2048]{1,0:T(8,128)(2,1)} copy(bf16[820,2048]{0,1:T(8,128)(2,1)} %bitcast.174) | data formatting | bytes 6717440 | tf_op jit(solution)/shard_map/dot_general | solution.py:73
  323.1 4.2 reshape.201
  328.6 4.5 collective-permute-start.4
  350.9 5.7 %collective-permute-start.6 = (f32[64,2,128]{2,1,0:T(2,128)S(1)}, f32[64,2,128]{2,1,0:T(2,128)S(1)}, u32[]{:S(2)}, u32[]{:S(2)}) collective-permute-start(f32[64,2,128]{2,1,0:T(2,128)S(1)} %add_add_fusion.2), channel_id=1, source_target_pairs={{0,1},{1,2},{2,3},{3,4},{4,5},{5,6},{6,7},{8,9},{9,10},{10,11},{11... | collective-permute-start | bytes 196616 | tf_op jit(solution)/shard_map/ppermute | solution.py:18
  360.4 122.4 %all-reduce.38.cloned.1.call-done = f32[2,3,5,164,128]{4,3,2,1,0:T(8,128)} async-done(((f32[2,3,5,164,128]{4,3,2,1,0:T(8,128)}), f32[2,3,5,164,128]{4,3,2,1,0:T(8,128)}) %all-reduce.38.cloned.1.call-update) | async-done | bytes 2519056 | tf_op jit(solution)/shard_map/psum | solution.py:216
  482.8 4.5 copy.36
  (201 shorter events, 79.9 us)
Async XLA Ops:
  7.2 133.5 %copy-start = (bf16[1,64,32,256]{3,2,1,0:T(8,128)(2,1)S(1)}, bf16[1,64,32,256]{3,2,1,0:T(8,128)(2,1)}, u32[]{:S(2)}) copy-start(bf16[1,64,32,256]{3,2,1,0:T(8,128)(2,1)} %param.8) | copy-start | bytes 3145732
  7.2 130.7 %all-gather.3.cloned.1.call-start = ((), (), s32[]{:S(2)}) async-start(), calls=%async_computation.1 | async-start | bytes 9437184 | tf_op jit(solution)/shard_map/all_gather | solution.py:174
  7.9 474.8 %all-reduce.38.cloned.1.call-start = ((), (), s32[]{:S(2)}) async-start(), calls=%async_computation | async-start | bytes 5160960 | tf_op jit(solution)/shard_map/psum | solution.py:216
  141.7 9.4 %copy-start.17 = (bf16[2,3,5,164,128]{4,0,3,2,1:T(2,128)(2,1)S(1)}, bf16[2,3,5,164,128]{4,0,3,2,1:T(2,128)(2,1)}, u32[]{:S(2)}) copy-start(bf16[2,3,5,164,128]{4,0,3,2,1:T(2,128)(2,1)} %param.13) | copy-start | bytes 3778564
  145.3 9.6 %collective-permute-start.1 = (bf16[64,2,164]{2,1,0:T(2,128)(2,1)S(1)}, bf16[64,2,164]{2,1,0:T(2,128)(2,1)S(1)}, u32[]{:S(2)}, u32[]{:S(2)}) collective-permute-start(bf16[64,2,164]{2,1,0:T(2,128)(2,1)S(1)} %get-tuple-element.76), channel_id=1, source_target_pairs={{1,0},{2,1},{3,2},{4,3},{5,4},{6,5},{7,6},{9,8},{10,9},{11,10},{12... | collective-permute-start | bytes 125960 | tf_op jit(solution)/shard_map/ppermute | solution.py:21
  146.6 8.3 %collective-permute-start = (bf16[64,2,164]{2,1,0:T(2,128)(2,1)S(1)}, bf16[64,2,164]{2,1,0:T(2,128)(2,1)S(1)}, u32[]{:S(2)}, u32[]{:S(2)}) collective-permute-start(bf16[64,2,164]{2,1,0:T(2,128)(2,1)S(1)} %get-tuple-element.77), channel_id=1, source_target_pairs={{0,1},{1,2},{2,3},{3,4},{4,5},{5,6},{6,7},{8,9},{9,10},{10,11},{11... | collective-permute-start | bytes 125960 | tf_op jit(solution)/shard_map/ppermute | solution.py:18
  166.1 12.1 %copy-start.34 = (bf16[1,1,5,164,128]{4,0,3,2,1:T(2,128)(2,1)S(1)}, bf16[1,1,5,164,128]{4,0,3,2,1:T(2,128)(2,1)}, u32[]{:S(2)}) copy-start(bf16[1,1,5,164,128]{4,0,3,2,1:T(2,128)(2,1)} %get-tuple-element.59) | copy-start | bytes 629764
  166.1 12.8 %copy-start.33 = (bf16[1,1,5,164,128]{4,0,3,2,1:T(2,128)(2,1)S(1)}, bf16[1,1,5,164,128]{4,0,3,2,1:T(2,128)(2,1)}, u32[]{:S(2)}) copy-start(bf16[1,1,5,164,128]{4,0,3,2,1:T(2,128)(2,1)} %get-tuple-element.60) | copy-start | bytes 629764
  170.6 12.0 %copy-start.46 = (bf16[64,32,128]{2,1,0:T(8,128)(2,1)}, bf16[64,32,128]{2,1,0:T(8,128)(2,1)S(1)}, u32[]{:S(2)}) copy-start(bf16[64,32,128]{2,1,0:T(8,128)(2,1)S(1)} %get-tuple-element.80) | copy-start | bytes 1572868
  170.6 9.8 %copy-start.32 = (bf16[1,1,5,164,128]{4,0,3,2,1:T(2,128)(2,1)S(1)}, bf16[1,1,5,164,128]{4,0,3,2,1:T(2,128)(2,1)}, u32[]{:S(2)}) copy-start(bf16[1,1,5,164,128]{4,0,3,2,1:T(2,128)(2,1)} %get-tuple-element.61) | copy-start | bytes 629764
  170.6 11.2 %copy-start.31 = (bf16[1,1,5,164,128]{4,0,3,2,1:T(2,128)(2,1)S(1)}, bf16[1,1,5,164,128]{4,0,3,2,1:T(2,128)(2,1)}, u32[]{:S(2)}) copy-start(bf16[1,1,5,164,128]{4,0,3,2,1:T(2,128)(2,1)} %get-tuple-element.62) | copy-start | bytes 629764
  171.2 48.4 %collective-permute-start.3 = (bf16[64,2,128]{2,1,0:T(2,128)(2,1)}, bf16[64,2,128]{2,1,0:T(2,128)(2,1)S(1)}, u32[]{:S(2)}, u32[]{:S(2)}) collective-permute-start(bf16[64,2,128]{2,1,0:T(2,128)(2,1)} %get-tuple-element.79), channel_id=1, source_target_pairs={{1,0},{2,1},{3,2},{4,3},{5,4},{6,5},{7,6},{9,8},{10,9},{11,10},{12... | collective-permute-start | bytes 98312 | tf_op jit(solution)/shard_map/ppermute | solution.py:21
  172.5 47.1 %collective-permute-start.2 = (bf16[64,2,128]{2,1,0:T(2,128)(2,1)}, bf16[64,2,128]{2,1,0:T(2,128)(2,1)}, u32[]{:S(2)}, u32[]{:S(2)}) collective-permute-start(bf16[64,2,128]{2,1,0:T(2,128)(2,1)} %get-tuple-element.78), channel_id=1, source_target_pairs={{0,1},{1,2},{2,3},{3,4},{4,5},{5,6},{6,7},{8,9},{9,10},{10,11},{11... | collective-permute-start | bytes 98312 | tf_op jit(solution)/shard_map/ppermute | solution.py:18
  178.2 5.0 %copy-start.30 = (bf16[1,1,5,164,128]{4,0,3,2,1:T(2,128)(2,1)S(1)}, bf16[1,1,5,164,128]{4,0,3,2,1:T(2,128)(2,1)}, u32[]{:S(2)}) copy-start(bf16[1,1,5,164,128]{4,0,3,2,1:T(2,128)(2,1)} %copy-done.29) | copy-start | bytes 629764
  179.0 5.0 %copy-start.28 = (bf16[1,1,5,164,128]{4,0,3,2,1:T(2,128)(2,1)S(1)}, bf16[1,1,5,164,128]{4,0,3,2,1:T(2,128)(2,1)}, u32[]{:S(2)}) copy-start(bf16[1,1,5,164,128]{4,0,3,2,1:T(2,128)(2,1)} %get-tuple-element.64) | copy-start | bytes 629764
  224.0 8.0 %copy-start.45 = (bf16[820,128,1]{1,0,2:T(8,128)(2,1)S(1)}, bf16[820,128,1]{1,0,2:T(8,128)(2,1)}, u32[]{:S(2)}) copy-start(bf16[820,128,1]{1,0,2:T(8,128)(2,1)} %reshape.226) | copy-start | bytes 629764
  237.9 47.4 %copy-start.11 = (f32[64,32,128]{2,1,0:T(8,128)}, f32[64,32,128]{2,1,0:T(8,128)S(1)}, u32[]{:S(2)}) copy-start(f32[64,32,128]{2,1,0:T(8,128)S(1)} %get-tuple-element.83) | copy-start | bytes 3145732
  250.6 4.5 copy-start.8
  250.6 4.5 copy-start.23
  250.6 4.5 copy-start.58
  269.7 6.1 %copy-start.52 = (bf16[5,128,128]{2,1,0:T(8,128)(2,1)S(1)}, bf16[5,128,128]{2,1,0:T(8,128)(2,1)}, u32[]{:S(2)}) copy-start(bf16[5,128,128]{2,1,0:T(8,128)(2,1)} %slice.398) | copy-start | bytes 491524
  275.0 5.6 %copy-start.39 = (bf16[64,32,128]{2,1,0:T(8,128)(2,1)}, bf16[64,32,128]{2,1,0:T(8,128)(2,1)S(1)}, u32[]{:S(2)}) copy-start(bf16[64,32,128]{2,1,0:T(8,128)(2,1)S(1)} %get-tuple-element.47) | copy-start | bytes 1572868
  323.1 10.1 %copy-start.48 = (bf16[5,128,128]{2,1,0:T(8,128)(2,1)S(1)}, bf16[5,128,128]{2,1,0:T(8,128)(2,1)}, u32[]{:S(2)}) copy-start(bf16[5,128,128]{2,1,0:T(8,128)(2,1)} %slice.423) | copy-start | bytes 491524
  327.3 14.4 %collective-permute-start.5 = (f32[64,2,128]{2,1,0:T(2,128)}, f32[64,2,128]{2,1,0:T(2,128)S(1)}, u32[]{:S(2)}, u32[]{:S(2)}) collective-permute-start(f32[64,2,128]{2,1,0:T(2,128)} %get-tuple-element.26), channel_id=1, source_target_pairs={{1,0},{2,1},{3,2},{4,3},{5,4},{6,5},{7,6},{9,8},{10,9},{11,10},{12... | collective-permute-start | bytes 196616 | tf_op jit(solution)/shard_map/ppermute | solution.py:21
  328.6 13.1 %collective-permute-start.4 = (f32[64,2,128]{2,1,0:T(2,128)S(1)}, f32[64,2,128]{2,1,0:T(2,128)S(1)}, u32[]{:S(2)}, u32[]{:S(2)}) collective-permute-start(f32[64,2,128]{2,1,0:T(2,128)S(1)} %get-tuple-element.25), channel_id=1, source_target_pairs={{0,1},{1,2},{2,3},{3,4},{4,5},{5,6},{6,7},{8,9},{9,10},{10,11},{11... | collective-permute-start | bytes 196616 | tf_op jit(solution)/shard_map/ppermute | solution.py:18
  349.4 9.0 %collective-permute-start.7 = (f32[64,2,128]{2,1,0:T(2,128)S(1)}, f32[64,2,128]{2,1,0:T(2,128)S(1)}, u32[]{:S(2)}, u32[]{:S(2)}) collective-permute-start(f32[64,2,128]{2,1,0:T(2,128)S(1)} %add_add_fusion.1), channel_id=1, source_target_pairs={{1,0},{2,1},{3,2},{4,3},{5,4},{6,5},{7,6},{9,8},{10,9},{11,10},{12... | collective-permute-start | bytes 196616 | tf_op jit(solution)/shard_map/ppermute | solution.py:21
  350.8 8.0 %copy-start.12 = (f32[64,32,128]{2,1,0:T(8,128)S(1)}, f32[64,32,128]{2,1,0:T(8,128)}, u32[]{:S(2)}) copy-start(f32[64,32,128]{2,1,0:T(8,128)} %copy-done.11) | copy-start | bytes 3145732
  350.9 8.0 %copy-start.14 = (f32[64,32,128]{2,1,0:T(8,128)S(1)}, f32[64,32,128]{2,1,0:T(8,128)}, u32[]{:S(2)}) copy-start(f32[64,32,128]{2,1,0:T(8,128)} %copy-done.13) | copy-start | bytes 3145732
  350.9 7.9 %copy-start.16 = (f32[64,36,128]{2,1,0:T(8,128)S(1)}, f32[64,36,128]{2,1,0:T(8,128)}, u32[]{:S(2)}) copy-start(f32[64,36,128]{2,1,0:T(8,128)} %pad_add_fusion) | copy-start | bytes 3538948
  350.9 7.9 %copy-start.26 = (f32[64,32,128]{2,1,0:T(8,128)S(1)}, f32[64,32,128]{2,1,0:T(8,128)}, u32[]{:S(2)}) copy-start(f32[64,32,128]{2,1,0:T(8,128)} %get-tuple-element.81) | copy-start | bytes 3145732
  350.9 7.9 %collective-permute-start.6 = (f32[64,2,128]{2,1,0:T(2,128)S(1)}, f32[64,2,128]{2,1,0:T(2,128)S(1)}, u32[]{:S(2)}, u32[]{:S(2)}) collective-permute-start(f32[64,2,128]{2,1,0:T(2,128)S(1)} %add_add_fusion.2), channel_id=1, source_target_pairs={{0,1},{1,2},{2,3},{3,4},{4,5},{5,6},{6,7},{8,9},{9,10},{10,11},{11... | collective-permute-start | bytes 196616 | tf_op jit(solution)/shard_map/ppermute | solution.py:18
  358.8 128.4 %copy-start.1 = (bf16[1,64,32,256]{3,2,1,0:T(8,128)(2,1)S(1)}, bf16[1,64,32,256]{3,2,1,0:T(8,128)(2,1)}, u32[]{:S(2)}) copy-start(bf16[1,64,32,256]{3,2,1,0:T(8,128)(2,1)} %param.8) | copy-start | bytes 3145732
  (38 other events, 80.8 us)
Sparse Core Ops, SparseCore 0:
  10.2 127.6 all-gather.2
  346.7 136.0 all-reduce.37
where the time goes:
time: 504 us; the launch traced here: 494 us
  waiting for transfers between devices  253 us (50%)
  local copies, waits for them, and re-layouts  141 us (28%)
  matrix products  41.8 us (8%)
  starting transfers between devices  25.7 us (5%)
  other arithmetic  17.8 us (4%)
  between operations  15.8 us (3%)
    all_gather x1, waiting for transfers between devices, on_device(): shards = lax.all_gather(right_block, 'blk', axis=1, tiled=True)  129 us
    psum x1, waiting for transfers between devices, on_device(): lax.psum(jnp.stack([first_grads, second_grads]), ('pair', 'blk'))  122 us
    concatenate x5, local copies, waits for them, and re-layouts, tap_stack(): jnp.concatenate([lax.slice_in_dim(padded, tap_id, tap_id + extent, axis=a...  40 us
    dot_general x4, local copies, waits for them, and re-layouts, conv_weight_grad(): lax.dot_general(flat_taps, flat_deltas, (((0,), (0,)), ((), ())), preferr...  24 us
    dot_general x6, matrix products, conv_apply(): jnp.dot(flat_taps, weight_taps.reshape(kernel_len * in_chan, out_chan), p...  23.4 us
    unnamed x133, local copies, waits for them, and re-layouts  22.1 us
    ppermute x4, starting transfers between devices, with_halo(): lax.ppermute(lax.slice_in_dim(block, block.shape[dim] - width, None, axis...  20.5 us
    another operation x4, local copies, waits for them, and re-layouts  17 us
  transfers between devices with their start and end apart: 10, of which 3 were waited for; matrix products, arithmetic and copies ran while one was open for 11% of the time, Pallas kernels for 0%

commit v1 on v0

--- a/solution.py
+++ b/solution.py
@@ -171,7 +171,21 @@
     empty_block = jnp.zeros_like(right_block)
     low_id = stripe - offset - 1
     high_id = stripe - offset
-    shards = lax.all_gather(right_block, "blk", axis=1, tiled=True)
+    ways, here, step = (lax.axis_size("blk"), lax.axis_index("blk"), right_block.shape[1])
+    shape = [n * ways if d == 1 else n for d, n in enumerate(right_block.shape)]
+    full = lax.dynamic_update_slice_in_dim(
+        jnp.zeros(shape, right_block.dtype), right_block, here * step, axis=1
+    )
+    going_up = going_down = right_block
+    for far in range(1, ways // 2 + 1):
+        going_up = lax.ppermute(going_up, "blk", [(d, (d + 1) % ways) for d in range(ways)])
+        full = lax.dynamic_update_slice_in_dim(full, going_up, (here - far) % ways * step, axis=1)
+        if 2 * far < ways:
+            going_down = lax.ppermute(going_down, "blk", [(d, (d - 1) % ways) for d in range(ways)])
+            full = lax.dynamic_update_slice_in_dim(
+                full, going_down, (here + far) % ways * step, axis=1
+            )
+    shards = full
     shard_cols = shards.shape[1]
 
     def pick_one(slot_block, block_id):

time: 504 us -> 537 us (1.065)
  starting transfers between devices: 25.7 us -> 44.7 us
  waiting for transfers between devices: 253 us -> 264 us
    ppermute x0 -> x7, waiting for transfers between devices: none -> 140 us  [the longest x4 140 us: on_device(): lax.ppermute(going_up, 'blk', [(d, (d + 1) % ways) for d in range(ways)])]
    all_gather x1 -> x0, waiting for transfers between devices: 129 us -> none  [on_device(): shards = lax.all_gather(right_block, 'blk', axis=1, tiled=True)]
    ppermute x0 -> x7, starting transfers between devices: none -> 19.6 us  [the longest x4 10.5 us: on_device(): lax.ppermute(going_up, 'blk', [(d, (d + 1) % ways) for d in range(ways)])]
    dynamic_update_slice x0 -> x8, local copies, waits for them, and re-layouts: none -> 5.65 us  [the longest x4 2.82 us: on_device(): lax.dynamic_update_slice_in_dim(full, going_up, (here - far) % ways * ste...]
    unnamed x133 -> x135, local copies, waits for them, and re-layouts: 22.1 us -> 20.9 us
  transfers between devices with their start and end apart: 10 -> 16, of which waited for: 3 -> 6; matrix products, arithmetic and copies ran while one was open for 11% -> 12% of each run, Pallas kernels for 0% -> 0%
where the time goes in v1:
time: 537 us; the launch traced here: 529 us
  waiting for transfers between devices  264 us (49%)
  local copies, waits for them, and re-layouts  146 us (27%)
  starting transfers between devices  44.7 us (8%)
  matrix products  41.8 us (8%)
  other arithmetic  16.2 us (3%)
  between operations  15.8 us (3%)
    ppermute x4, waiting for transfers between devices, on_device(): lax.ppermute(going_up, 'blk', [(d, (d + 1) % ways) for d in range(ways)])  140 us
    psum x1, waiting for transfers between devices, on_device(): lax.psum(jnp.stack([first_grads, second_grads]), ('pair', 'blk'))  123 us
    concatenate x5, local copies, waits for them, and re-layouts, tap_stack(): jnp.concatenate([lax.slice_in_dim(padded, tap_id, tap_id + extent, axis=a...  40 us
    dot_general x4, local copies, waits for them, and re-layouts, conv_weight_grad(): lax.dot_general(flat_taps, flat_deltas, (((0,), (0,)), ((), ())), preferr...  24.1 us
    dot_general x6, matrix products, conv_apply(): jnp.dot(flat_taps, weight_taps.reshape(kernel_len * in_chan, out_chan), p...  23.4 us
    unnamed x135, local copies, waits for them, and re-layouts  20.9 us
    ppermute x4, starting transfers between devices, with_halo(): lax.ppermute(lax.slice_in_dim(block, block.shape[dim] - width, None, axis...  19.9 us
    another operation x4, local copies, waits for them, and re-layouts  17.2 us
  transfers between devices with their start and end apart: 16, of which 6 were waited for; matrix products, arithmetic and copies ran while one was open for 12% of the time, Pallas kernels for 0%

profile of v1, /device:TPU:0, one launch (start us, length us, event | category | flops | bytes accessed | tf_op | source)
XLA Modules:
  0.0 528.9 jit_solution(12100564626631081212)
XLA Ops:
  10.2 3.1 collective-permute-start.1
  13.4 42.1 %collective-permute-done = bf16[64,32,256]{2,1,0:T(8,128)(2,1)S(1)} collective-permute-done((bf16[64,32,256]{2,1,0:T(8,128)(2,1)}, bf16[64,32,256]{2,1,0:T(8,128)(2,1)S(1)}, u32[]{:S(2)}, u32[]{:S(2)}) %collective-permute-start) | collective-permute-done | bytes 1048608 | tf_op jit(solution)/shard_map/ppermute | solution.py:181
  57.8 3.0 collective-permute-start.3
  60.9 41.0 %collective-permute-done.2 = bf16[64,32,256]{2,1,0:T(8,128)(2,1)} collective-permute-done((bf16[64,32,256]{2,1,0:T(8,128)(2,1)S(1)}, bf16[64,32,256]{2,1,0:T(8,128)(2,1)}, u32[]{:S(2)}, u32[]{:S(2)}) %collective-permute-start.2) | collective-permute-done | bytes 1048608 | tf_op jit(solution)/shard_map/ppermute | solution.py:181
  104.4 3.0 collective-permute-start.5
  108.2 39.8 %collective-permute-done.4 = bf16[64,32,256]{2,1,0:T(8,128)(2,1)} collective-permute-done((bf16[64,32,256]{2,1,0:T(8,128)(2,1)}, bf16[64,32,256]{2,1,0:T(8,128)(2,1)}, u32[]{:S(2)}, u32[]{:S(2)}) %collective-permute-start.4) | collective-permute-done | bytes 1048608 | tf_op jit(solution)/shard_map/ppermute | solution.py:181
  157.1 17.2 %collective-permute-done.6 = bf16[64,32,256]{2,1,0:T(8,128)(2,1)S(1)} collective-permute-done((bf16[64,32,256]{2,1,0:T(8,128)(2,1)}, bf16[64,32,256]{2,1,0:T(8,128)(2,1)S(1)}, u32[]{:S(2)}, u32[]{:S(2)}) %collective-permute-start.6) | collective-permute-done | bytes 1048608 | tf_op jit(solution)/shard_map/ppermute | solution.py:181
  181.5 5.1 collective-permute-start.7
  193.9 7.6 %concatenate.75 = bf16[64,32,820]{2,1,0:T(8,128)(2,1)} concatenate(bf16[64,32,164]{2,1,0:T(8,128)(2,1)} %get-tuple-element.86, bf16[64,32,164]{2,1,0:T(8,128)(2,1)} %get-tuple-element.87, bf16[64,32,128]{2,1,0:T(8,128)(2,1)S(1)} %bitcast.175, bf16[64,32,36]{2,1,0:T(8,128)(2,1)S(1)} %copy.20, bf16[64,32,164]{2,1,0:T(8,128)(2,1)S(1)} %get-tuple-element.56, ...), dimensions={2} | concatenate | bytes 6717440 | tf_op jit(solution)/shard_map/concatenate | solution.py:46
  201.5 4.4 fusion.34
  208.0 5.3 %collective-permute-start.9 = (bf16[64,2,128]{2,1,0:T(2,128)(2,1)}, bf16[64,2,128]{2,1,0:T(2,128)(2,1)}, u32[]{:S(2)}, u32[]{:S(2)}) collective-permute-start(bf16[64,2,128]{2,1,0:T(2,128)(2,1)} %get-tuple-element.78), channel_id=1, source_target_pairs={{0,1},{1,2},{2,3},{3,4},{4,5},{5,6},{6,7},{8,9},{9,10},{10,11},{11... | collective-permute-start | bytes 98312 | tf_op jit(solution)/shard_map/ppermute | solution.py:18
  236.8 7.6 %concatenate.90 = bf16[2048,820]{1,0:T(8,128)(2,1)} concatenate(bf16[2048,164]{1,0:T(8,128)(2,1)} %bitcast.183, bf16[2048,164]{1,0:T(8,128)(2,1)} %bitcast.184, bf16[2048,128]{1,0:T(8,128)(2,1)S(1)} %bitcast.176, bf16[2048,36]{1,0:T(8,128)(2,1)S(1)} %bitcast.171, bf16[2048,164]{1,0:T(8,128)(2,1)S(1)} %bitcast.182, bf16[2048,164]{1,0:T(8,128)(2,1)S(1)} %bitcast.181), dimensions={1} | concatenate | bytes 6717440 | tf_op jit(solution)/shard_map/concatenate | solution.py:46
  244.4 6.0 %copy.32 = bf16[820,2048]{1,0:T(8,128)(2,1)} copy(bf16[820,2048]{0,1:T(8,128)(2,1)} %bitcast.180) | data formatting | bytes 6717440 | tf_op jit(solution)/shard_map/dot_general | solution.py:73
  250.4 4.2 reshape.193
  259.1 8.0 %concatenate.79 = bf16[64,32,820]{2,1,0:T(8,128)(2,1)} concatenate(bf16[64,32,164]{2,1,0:T(8,128)(2,1)} %get-tuple-element.54, bf16[64,32,164]{2,1,0:T(8,128)(2,1)} %get-tuple-element.53, bf16[64,32,164]{2,1,0:T(8,128)(2,1)} %get-tuple-element.52, bf16[64,32,164]{2,1,0:T(8,128)(2,1)S(1)} %get-tuple-element.51, bf16[64,32,164]{2,1,0:T(8,128)(2,1)S(1)} %get-tuple-element.50), dimensions={2} | concatenate | bytes 6717440 | tf_op jit(solution)/shard_map/concatenate | solution.py:46
  267.0 3.4 fusion.17
  277.3 8.3 %concatenate.81 = bf16[64,32,820]{2,1,0:T(8,128)(2,1)} concatenate(bf16[64,32,164]{2,1,0:T(8,128)(2,1)} %get-tuple-element.73, bf16[64,32,164]{2,1,0:T(8,128)(2,1)} %get-tuple-element.71, bf16[64,32,128]{2,1,0:T(8,128)(2,1)} %copy-done.22, bf16[64,32,36]{2,1,0:T(8,128)(2,1)S(1)} %copy.20, bf16[64,32,164]{2,1,0:T(8,128)(2,1)} %get-tuple-element.72, ...), dimensions={2} | concatenate | bytes 6717440 | tf_op jit(solution)/shard_map/concatenate | solution.py:46
  285.6 4.5 fusion.16
  290.1 3.3 fusion.44
  296.1 8.6 %concatenate.83 = bf16[64,32,820]{2,1,0:T(8,128)(2,1)} concatenate(bf16[64,32,164]{2,1,0:T(8,128)(2,1)} %get-tuple-element.69, bf16[64,32,164]{2,1,0:T(8,128)(2,1)} %get-tuple-element.68, bf16[64,32,164]{2,1,0:T(8,128)(2,1)} %get-tuple-element.67, bf16[64,32,164]{2,1,0:T(8,128)(2,1)} %get-tuple-element.66, bf16[64,32,164]{2,1,0:T(8,128)(2,1)} %get-tuple-element.65), dimensions={2} | concatenate | bytes 6717440 | tf_op jit(solution)/shard_map/concatenate | solution.py:46
  304.7 5.3 %fusion.48 = (bf16[64,32,128]{2,1,0:T(8,128)(2,1)S(1)}, bf16[64,32,128]{2,1,0:T(8,128)(2,1)S(1)}, bf16[1,64,32,128]{3,2,1,0:T(8,128)(2,1)}) fusion(f32[64,32,128]{2,1,0:T(8,128)} %fusion.16, bf16[64,32,128]{2,1,0:T(8,128)(2,1)S(1)} %copy-done.23, f32[1,64,32,128]{3,2,1,0:T(8,128)} %param.14, bf16[1,3,64,32,128]{4,3,2,1,0:T(8,128)(2,1)} %param.12, ...), kind=kOutput, calls=%fused_computation.80 | convolution fusion | flops 434634752 | bytes 8287232 | tf_op jit(solution)/shard_map/dot_general | solution.py:59
  325.7 6.0 %copy.35 = bf16[820,2048]{1,0:T(8,128)(2,1)} copy(bf16[820,2048]{0,1:T(8,128)(2,1)} %bitcast.179) | data formatting | bytes 6717440 | tf_op jit(solution)/shard_map/dot_general | solution.py:73
  331.7 4.2 reshape.208
  335.9 6.0 %copy.34 = bf16[820,2048]{1,0:T(8,128)(2,1)} copy(bf16[820,2048]{0,1:T(8,128)(2,1)} %bitcast.178) | data formatting | bytes 6717440 | tf_op jit(solution)/shard_map/dot_general | solution.py:73
  341.9 4.6 reshape.204
  346.5 4.0 convolution_bitcast_fusion.1
  352.3 6.0 %copy.33 = bf16[820,2048]{1,0:T(8,128)(2,1)} copy(bf16[820,2048]{0,1:T(8,128)(2,1)} %bitcast.172) | data formatting | bytes 6717440 | tf_op jit(solution)/shard_map/dot_general | solution.py:73
  358.4 4.2 reshape.201
  363.9 4.5 collective-permute-start.11
  385.1 5.0 collective-permute-start.13
  393.9 123.5 %all-reduce.38.cloned.1.call-done = f32[2,3,5,164,128]{4,3,2,1,0:T(8,128)} async-done(((f32[2,3,5,164,128]{4,3,2,1,0:T(8,128)}), f32[2,3,5,164,128]{4,3,2,1,0:T(8,128)}) %all-reduce.38.cloned.1.call-update) | async-done | bytes 2519056 | tf_op jit(solution)/shard_map/psum | solution.py:230
  517.4 4.5 copy.36
  (223 shorter events, 109.7 us)
Async XLA Ops:
  7.2 168.4 %copy-start = (bf16[1,64,32,256]{3,2,1,0:T(8,128)(2,1)S(1)}, bf16[1,64,32,256]{3,2,1,0:T(8,128)(2,1)}, u32[]{:S(2)}) copy-start(bf16[1,64,32,256]{3,2,1,0:T(8,128)(2,1)} %param.8) | copy-start | bytes 3145732
  7.2 510.2 %all-reduce.38.cloned.1.call-start = ((), (), s32[]{:S(2)}) async-start(), calls=%async_computation | async-start | bytes 5160960 | tf_op jit(solution)/shard_map/psum | solution.py:230
  7.2 48.2 %collective-permute-start = (bf16[64,32,256]{2,1,0:T(8,128)(2,1)}, bf16[64,32,256]{2,1,0:T(8,128)(2,1)S(1)}, u32[]{:S(2)}, u32[]{:S(2)}) collective-permute-start(bf16[64,32,256]{2,1,0:T(8,128)(2,1)} %bitcast.191), channel_id=1, source_target_pairs={{0,1},{1,2},{2,3},{3,4},{4,5},{5,6},{6,7},{7,0},{8,9},{9,10},{10,1... | collective-permute-start | bytes 3145736 | tf_op jit(solution)/shard_map/ppermute | solution.py:181
  10.2 47.6 %collective-permute-start.1 = (bf16[64,32,256]{2,1,0:T(8,128)(2,1)}, bf16[64,32,256]{2,1,0:T(8,128)(2,1)S(1)}, u32[]{:S(2)}, u32[]{:S(2)}) collective-permute-start(bf16[64,32,256]{2,1,0:T(8,128)(2,1)} %bitcast.192), channel_id=1, source_target_pairs={{0,7},{1,0},{2,1},{3,2},{4,3},{5,4},{6,5},{7,6},{8,15},{9,8},{10,9... | collective-permute-start | bytes 3145736 | tf_op jit(solution)/shard_map/ppermute | solution.py:184
  55.5 46.4 %collective-permute-start.2 = (bf16[64,32,256]{2,1,0:T(8,128)(2,1)S(1)}, bf16[64,32,256]{2,1,0:T(8,128)(2,1)}, u32[]{:S(2)}, u32[]{:S(2)}) collective-permute-start(bf16[64,32,256]{2,1,0:T(8,128)(2,1)S(1)} %collective-permute-done), channel_id=1, source_target_pairs={{0,1},{1,2},{2,3},{3,4},{4,5},{5,6},{6,7},{7,0},{8,9},{9,10},{10,1... | collective-permute-start | bytes 3145736 | tf_op jit(solution)/shard_map/ppermute | solution.py:181
  57.8 46.6 %collective-permute-start.3 = (bf16[64,32,256]{2,1,0:T(8,128)(2,1)S(1)}, bf16[64,32,256]{2,1,0:T(8,128)(2,1)}, u32[]{:S(2)}, u32[]{:S(2)}) collective-permute-start(bf16[64,32,256]{2,1,0:T(8,128)(2,1)S(1)} %collective-permute-done.1), channel_id=1, source_target_pairs={{0,7},{1,0},{2,1},{3,2},{4,3},{5,4},{6,5},{7,6},{8,15},{9,8},{10,9... | collective-permute-start | bytes 3145736 | tf_op jit(solution)/shard_map/ppermute | solution.py:184
  101.8 46.2 %collective-permute-start.4 = (bf16[64,32,256]{2,1,0:T(8,128)(2,1)}, bf16[64,32,256]{2,1,0:T(8,128)(2,1)}, u32[]{:S(2)}, u32[]{:S(2)}) collective-permute-start(bf16[64,32,256]{2,1,0:T(8,128)(2,1)} %collective-permute-done.2), channel_id=1, source_target_pairs={{0,1},{1,2},{2,3},{3,4},{4,5},{5,6},{6,7},{7,0},{8,9},{9,10},{10,1... | collective-permute-start | bytes 3145736 | tf_op jit(solution)/shard_map/ppermute | solution.py:181
  104.4 51.4 %collective-permute-start.5 = (bf16[64,32,256]{2,1,0:T(8,128)(2,1)}, bf16[64,32,256]{2,1,0:T(8,128)(2,1)}, u32[]{:S(2)}, u32[]{:S(2)}) collective-permute-start(bf16[64,32,256]{2,1,0:T(8,128)(2,1)} %collective-permute-done.3), channel_id=1, source_target_pairs={{0,7},{1,0},{2,1},{3,2},{4,3},{5,4},{6,5},{7,6},{8,15},{9,8},{10,9... | collective-permute-start | bytes 3145736 | tf_op jit(solution)/shard_map/ppermute | solution.py:184
  108.2 43.3 %copy-start.45 = (bf16[1,64,32,256]{3,2,1,0:T(8,128)(2,1)S(1)}, bf16[1,64,32,256]{3,2,1,0:T(8,128)(2,1)}, u32[]{:S(2)}) copy-start(bf16[1,64,32,256]{3,2,1,0:T(8,128)(2,1)} %param.9) | copy-start | bytes 3145732
  148.0 26.3 %collective-permute-start.6 = (bf16[64,32,256]{2,1,0:T(8,128)(2,1)}, bf16[64,32,256]{2,1,0:T(8,128)(2,1)S(1)}, u32[]{:S(2)}, u32[]{:S(2)}) collective-permute-start(bf16[64,32,256]{2,1,0:T(8,128)(2,1)} %collective-permute-done.4), channel_id=1, source_target_pairs={{0,1},{1,2},{2,3},{3,4},{4,5},{5,6},{6,7},{7,0},{8,9},{9,10},{10,1... | collective-permute-start | bytes 3145736 | tf_op jit(solution)/shard_map/ppermute | solution.py:181
  176.6 9.9 %copy-start.17 = (bf16[2,3,5,164,128]{4,0,3,2,1:T(2,128)(2,1)S(1)}, bf16[2,3,5,164,128]{4,0,3,2,1:T(2,128)(2,1)}, u32[]{:S(2)}) copy-start(bf16[2,3,5,164,128]{4,0,3,2,1:T(2,128)(2,1)} %param.13) | copy-start | bytes 3778564
  180.2 10.1 %collective-permute-start.8 = (bf16[64,2,164]{2,1,0:T(2,128)(2,1)S(1)}, bf16[64,2,164]{2,1,0:T(2,128)(2,1)S(1)}, u32[]{:S(2)}, u32[]{:S(2)}) collective-permute-start(bf16[64,2,164]{2,1,0:T(2,128)(2,1)S(1)} %get-tuple-element.76), channel_id=1, source_target_pairs={{1,0},{2,1},{3,2},{4,3},{5,4},{6,5},{7,6},{9,8},{10,9},{11,10},{12... | collective-permute-start | bytes 125960 | tf_op jit(solution)/shard_map/ppermute | solution.py:21
  181.5 8.8 %collective-permute-start.7 = (bf16[64,2,164]{2,1,0:T(2,128)(2,1)S(1)}, bf16[64,2,164]{2,1,0:T(2,128)(2,1)S(1)}, u32[]{:S(2)}, u32[]{:S(2)}) collective-permute-start(bf16[64,2,164]{2,1,0:T(2,128)(2,1)S(1)} %get-tuple-element.77), channel_id=1, source_target_pairs={{0,1},{1,2},{2,3},{3,4},{4,5},{5,6},{6,7},{8,9},{9,10},{10,11},{11... | collective-permute-start | bytes 125960 | tf_op jit(solution)/shard_map/ppermute | solution.py:18
  201.5 11.7 %copy-start.34 = (bf16[1,1,5,164,128]{4,0,3,2,1:T(2,128)(2,1)S(1)}, bf16[1,1,5,164,128]{4,0,3,2,1:T(2,128)(2,1)}, u32[]{:S(2)}) copy-start(bf16[1,1,5,164,128]{4,0,3,2,1:T(2,128)(2,1)} %get-tuple-element.59) | copy-start | bytes 629764
  201.5 12.5 %copy-start.33 = (bf16[1,1,5,164,128]{4,0,3,2,1:T(2,128)(2,1)S(1)}, bf16[1,1,5,164,128]{4,0,3,2,1:T(2,128)(2,1)}, u32[]{:S(2)}) copy-start(bf16[1,1,5,164,128]{4,0,3,2,1:T(2,128)(2,1)} %get-tuple-element.60) | copy-start | bytes 629764
  206.0 13.1 %copy-start.47 = (bf16[64,32,128]{2,1,0:T(8,128)(2,1)}, bf16[64,32,128]{2,1,0:T(8,128)(2,1)S(1)}, u32[]{:S(2)}) copy-start(bf16[64,32,128]{2,1,0:T(8,128)(2,1)S(1)} %get-tuple-element.80) | copy-start | bytes 1572868
  206.0 9.5 %copy-start.32 = (bf16[1,1,5,164,128]{4,0,3,2,1:T(2,128)(2,1)S(1)}, bf16[1,1,5,164,128]{4,0,3,2,1:T(2,128)(2,1)}, u32[]{:S(2)}) copy-start(bf16[1,1,5,164,128]{4,0,3,2,1:T(2,128)(2,1)} %get-tuple-element.61) | copy-start | bytes 629764
  206.0 10.9 %copy-start.31 = (bf16[1,1,5,164,128]{4,0,3,2,1:T(2,128)(2,1)S(1)}, bf16[1,1,5,164,128]{4,0,3,2,1:T(2,128)(2,1)}, u32[]{:S(2)}) copy-start(bf16[1,1,5,164,128]{4,0,3,2,1:T(2,128)(2,1)} %get-tuple-element.62) | copy-start | bytes 629764
  206.0 12.3 %copy-start.30 = (bf16[1,1,5,164,128]{4,0,3,2,1:T(2,128)(2,1)S(1)}, bf16[1,1,5,164,128]{4,0,3,2,1:T(2,128)(2,1)}, u32[]{:S(2)}) copy-start(bf16[1,1,5,164,128]{4,0,3,2,1:T(2,128)(2,1)} %copy-done.29) | copy-start | bytes 629764
  206.7 48.0 %collective-permute-start.10 = (bf16[64,2,128]{2,1,0:T(2,128)(2,1)}, bf16[64,2,128]{2,1,0:T(2,128)(2,1)S(1)}, u32[]{:S(2)}, u32[]{:S(2)}) collective-permute-start(bf16[64,2,128]{2,1,0:T(2,128)(2,1)} %get-tuple-element.79), channel_id=1, source_target_pairs={{1,0},{2,1},{3,2},{4,3},{5,4},{6,5},{7,6},{9,8},{10,9},{11,10},{12... | collective-permute-start | bytes 98312 | tf_op jit(solution)/shard_map/ppermute | solution.py:21
  208.0 46.7 %collective-permute-start.9 = (bf16[64,2,128]{2,1,0:T(2,128)(2,1)}, bf16[64,2,128]{2,1,0:T(2,128)(2,1)}, u32[]{:S(2)}, u32[]{:S(2)}) collective-permute-start(bf16[64,2,128]{2,1,0:T(2,128)(2,1)} %get-tuple-element.78), channel_id=1, source_target_pairs={{0,1},{1,2},{2,3},{3,4},{4,5},{5,6},{6,7},{8,9},{9,10},{10,11},{11... | collective-permute-start | bytes 98312 | tf_op jit(solution)/shard_map/ppermute | solution.py:18
  259.1 8.0 %copy-start.46 = (bf16[820,128,1]{1,0,2:T(8,128)(2,1)S(1)}, bf16[820,128,1]{1,0,2:T(8,128)(2,1)}, u32[]{:S(2)}) copy-start(bf16[820,128,1]{1,0,2:T(8,128)(2,1)} %reshape.217) | copy-start | bytes 629764
  272.9 47.4 %copy-start.11 = (f32[64,32,128]{2,1,0:T(8,128)}, f32[64,32,128]{2,1,0:T(8,128)S(1)}, u32[]{:S(2)}) copy-start(f32[64,32,128]{2,1,0:T(8,128)S(1)} %get-tuple-element.83) | copy-start | bytes 3145732
  358.4 10.1 %copy-start.49 = (bf16[5,128,128]{2,1,0:T(8,128)(2,1)S(1)}, bf16[5,128,128]{2,1,0:T(8,128)(2,1)}, u32[]{:S(2)}) copy-start(bf16[5,128,128]{2,1,0:T(8,128)(2,1)} %slice.423) | copy-start | bytes 491524
  362.6 14.4 %collective-permute-start.12 = (f32[64,2,128]{2,1,0:T(2,128)}, f32[64,2,128]{2,1,0:T(2,128)S(1)}, u32[]{:S(2)}, u32[]{:S(2)}) collective-permute-start(f32[64,2,128]{2,1,0:T(2,128)} %get-tuple-element.26), channel_id=1, source_target_pairs={{1,0},{2,1},{3,2},{4,3},{5,4},{6,5},{7,6},{9,8},{10,9},{11,10},{12... | collective-permute-start | bytes 196616 | tf_op jit(solution)/shard_map/ppermute | solution.py:21
  363.9 13.1 %collective-permute-start.11 = (f32[64,2,128]{2,1,0:T(2,128)S(1)}, f32[64,2,128]{2,1,0:T(2,128)S(1)}, u32[]{:S(2)}, u32[]{:S(2)}) collective-permute-start(f32[64,2,128]{2,1,0:T(2,128)S(1)} %get-tuple-element.25), channel_id=1, source_target_pairs={{0,1},{1,2},{2,3},{3,4},{4,5},{5,6},{6,7},{8,9},{9,10},{10,11},{11... | collective-permute-start | bytes 196616 | tf_op jit(solution)/shard_map/ppermute | solution.py:18
  383.6 8.2 %collective-permute-start.14 = (f32[64,2,128]{2,1,0:T(2,128)S(1)}, f32[64,2,128]{2,1,0:T(2,128)S(1)}, u32[]{:S(2)}, u32[]{:S(2)}) collective-permute-start(f32[64,2,128]{2,1,0:T(2,128)S(1)} %add_add_fusion.1), channel_id=1, source_target_pairs={{1,0},{2,1},{3,2},{4,3},{5,4},{6,5},{7,6},{9,8},{10,9},{11,10},{12... | collective-permute-start | bytes 196616 | tf_op jit(solution)/shard_map/ppermute | solution.py:21
  385.1 7.3 %copy-start.12 = (f32[64,32,128]{2,1,0:T(8,128)S(1)}, f32[64,32,128]{2,1,0:T(8,128)}, u32[]{:S(2)}) copy-start(f32[64,32,128]{2,1,0:T(8,128)} %copy-done.11) | copy-start | bytes 3145732
  385.1 7.2 %copy-start.14 = (f32[64,32,128]{2,1,0:T(8,128)S(1)}, f32[64,32,128]{2,1,0:T(8,128)}, u32[]{:S(2)}) copy-start(f32[64,32,128]{2,1,0:T(8,128)} %copy-done.13) | copy-start | bytes 3145732
  385.1 7.2 %copy-start.16 = (f32[64,36,128]{2,1,0:T(8,128)S(1)}, f32[64,36,128]{2,1,0:T(8,128)}, u32[]{:S(2)}) copy-start(f32[64,36,128]{2,1,0:T(8,128)} %pad_add_fusion) | copy-start | bytes 3538948
  385.1 7.2 %collective-permute-start.13 = (f32[64,2,128]{2,1,0:T(2,128)S(1)}, f32[64,2,128]{2,1,0:T(2,128)S(1)}, u32[]{:S(2)}, u32[]{:S(2)}) collective-permute-start(f32[64,2,128]{2,1,0:T(2,128)S(1)} %add_add_fusion.2), channel_id=1, source_target_pairs={{0,1},{1,2},{2,3},{3,4},{4,5},{5,6},{6,7},{8,9},{9,10},{10,11},{11... | collective-permute-start | bytes 196616 | tf_op jit(solution)/shard_map/ppermute | solution.py:18
  392.4 129.5 %copy-start.1 = (bf16[1,64,32,256]{3,2,1,0:T(8,128)(2,1)S(1)}, bf16[1,64,32,256]{3,2,1,0:T(8,128)(2,1)}, u32[]{:S(2)}) copy-start(bf16[1,64,32,256]{3,2,1,0:T(8,128)(2,1)} %param.8) | copy-start | bytes 3145732
  (45 other events, 119.3 us)
Sparse Core Ops, SparseCore 0:
  380.9 136.3 all-reduce.37
